TPU v7x, 256 devices: a whole 4x4x8 slice. The times are simulated.
256 devices in a mesh: row: 16 (over x, y_lo, core), col: 8 (over z), slab: 2 (over y_hi).
Axes of the slice: x: 4, y: 4 (y_hi: 2, y_lo: 2; y = y_hi * 2 + y_lo), z: 8, core: 2. Of those that a mesh axis runs over, the one named last changes fastest.
Arguments:
- fields: bfloat16 [2, 16384, 1024], P(None, ('row', 'col', 'slab')), may hold values from -0.8984375 to 0.8984375
Outputs:
- gram: float32 [2, 16384, 16384], P(None, ('row', 'slab'), 'col')
All inputs are finite; a program needn't handle non-finite values.
Results may differ from a plain program's by a relative error of at most 0.01.
Values may be sent and summed in bfloat16 or wider, within the bound.
A program may use at most 64 MiB of HBM per device.

v0:
```python
import jax
import jax.numpy as jnp
from jax import lax
from jax.sharding import PartitionSpec as P


def pair_terms(left_real, left_imag, piece):
    right_real = jnp.concatenate([piece[0], piece[1]], axis=1)
    right_imag = jnp.concatenate([piece[1], piece[0]], axis=1)
    dims = (((1,), (1,)), ((), ()))
    real = lax.dot_general(left_real, right_real, dims, preferred_element_type=jnp.float32)
    imag = lax.dot_general(left_imag, right_imag, dims, preferred_element_type=jnp.float32)
    return jnp.stack([real, imag])


def body(fields):
    local = lax.all_to_all(fields, "slab", split_axis=2, concat_axis=1, tiled=True)
    row_block = lax.all_gather(local, "col", axis=1, tiled=True)
    left_real = jnp.concatenate([row_block[0], row_block[1]], axis=1)
    left_imag = jnp.concatenate([row_block[0], -row_block[1]], axis=1)
    column_set = lax.all_gather(local, "row", axis=1, tiled=True)
    terms = pair_terms(left_real, left_imag, column_set)
    gram = lax.psum_scatter(
        terms.astype(jnp.bfloat16), "slab", scatter_dimension=1, tiled=True
    ).astype(jnp.float32)
    return gram


def solution(mesh):
    placed = (P(None, ("row", "col", "slab"), None),)
    return jax.shard_map(
        body, mesh=mesh, in_specs=placed, out_specs=P(None, ("row", "slab"), "col"), check_vma=False
    )
```

profile of v0, /device:TPU:1, one launch (start us, length us, event | category | flops | bytes accessed | tf_op | source)
XLA Modules:
  0.0 242.6 jit_solution(3190334933049715580)
XLA Ops:
  6.5 0.0 all-gather.3.cloned.1.call-start
  6.5 1.3 copy.3
  7.8 0.4 reshape
  8.2 10.3 %all_to_all.18 = bf16[2,2,32768]{2,1,0:T(2,128)(2,1)S(1)} all-to-all(bf16[2,2,32768]{2,1,0:T(2,128)(2,1)S(1)} %reshape), channel_id=1, replica_groups=mesh['row'=16,'col'=8,'slab'=2] {'slab'}, dimensions={0} | all-to-all | bytes 524288 | tf_op jit(solution)/shard_map/all_to_all | solution.py:17
  18.6 0.3 reshape.1
  18.9 1.0 copy.5
  19.9 0.0 all-gather.3.cloned.1.call-update
  19.9 0.0 all-gather.5.cloned.1.call-start
  20.0 0.7 all-gather.5.cloned.1.call-update
  20.7 0.0 reduce-scatter.2.cloned.1.call-start
  20.7 38.7 %all-gather.3.cloned.1.call-done = bf16[2,1024,512]{2,1,0:T(8,128)(2,1)} async-done(((bf16[2,128,512]{2,1,0:T(8,128)(2,1)}), bf16[2,1024,512]{2,1,0:T(8,128)(2,1)}) %all-gather.3.cloned.1.call-update) | async-done | bytes 2097168 | tf_op jit(solution)/shard_map/all_gather | solution.py:18
  59.4 1.3 fusion.16
  60.7 2.6 %slice_bitcast_fusion.2 = (bf16[1024,512]{1,0:T(8,128)(2,1)}, bf16[1024,512]{1,0:T(8,128)(2,1)S(1)}) fusion(bf16[2,1024,512]{2,1,0:T(8,128)(2,1)} %all-gather.3.cloned.1.call-done), kind=kLoop, calls=%fused_computation.17 | loop fusion | bytes 4194304 | tf_op jit(solution)/shard_map/squeeze | solution.py:19
  63.3 40.4 %all-gather.5.cloned.1.call-done = bf16[2,2048,512]{2,1,0:T(8,128)(2,1)} async-done(((bf16[2,128,512]{2,1,0:T(8,128)(2,1)}), bf16[2,2048,512]{2,1,0:T(8,128)(2,1)}) %all-gather.5.cloned.1.call-update) | async-done | bytes 4194320 | tf_op jit(solution)/shard_map/all_gather | solution.py:21
  103.8 0.0 copy-start
  103.8 2.6 %slice_bitcast_fusion = (bf16[2048,512]{1,0:T(8,128)(2,1)S(1)}, bf16[2048,512]{1,0:T(8,128)(2,1)S(1)}) fusion(bf16[2,2048,512]{2,1,0:T(8,128)(2,1)} %all-gather.5.cloned.1.call-done), kind=kLoop, calls=%fused_computation.13 | loop fusion | bytes 8388608 | tf_op jit(solution)/shard_map/squeeze | solution.py:8
  106.3 0.0 copy-done
  106.3 4.8 %convert_bitcast_fusion.1 = bf16[1,1024,2048]{2,1,0:T(8,128)(2,1)S(1)} fusion(bf16[2048,512]{1,0:T(8,128)(2,1)S(1)} %get-tuple-element.5, bf16[2048,512]{1,0:T(8,128)(2,1)S(1)} %get-tuple-element.6, bf16[1024,512]{1,0:T(8,128)(2,1)S(1)} %get-tuple-element.8, bf16[1024,512]{1,0:T(8,128)(2,1)S(1)} %copy-done), kind=kOutput, calls=%fused_computation.10 | convolution fusion | flops 4309647360 | bytes 10485760 | tf_op jit(solution)/shard_map/dot_general | solution.py:11
  111.1 6.1 %convert_bitcast_fusion = bf16[1,1024,2048]{2,1,0:T(8,128)(2,1)} fusion(bf16[2048,512]{1,0:T(8,128)(2,1)S(1)} %get-tuple-element.6, bf16[2048,512]{1,0:T(8,128)(2,1)S(1)} %get-tuple-element.5, bf16[1024,512]{1,0:T(8,128)(2,1)S(1)} %get-tuple-element.8, bf16[1024,512]{1,0:T(8,128)(2,1)S(1)} %fusion.16), kind=kOutput, calls=%fused_computation.9 | convolution fusion | flops 4309647360 | bytes 10485760 | tf_op jit(solution)/shard_map/dot_general | solution.py:12
  117.3 6.3 %pad_maximum_fusion = bf16[2,1024,2048]{2,1,0:T(8,128)(2,1)} fusion(bf16[1,1024,2048]{2,1,0:T(8,128)(2,1)} %convert_bitcast_fusion, bf16[1,1024,2048]{2,1,0:T(8,128)(2,1)S(1)} %convert_bitcast_fusion.1), kind=kLoop, calls=%fused_computation | loop fusion | flops 4194304 | bytes 16777216 | tf_op jit(solution)/shard_map/stack | solution.py:13
  123.6 0.0 reduce-scatter.2.cloned.1.call-update
  123.6 105.7 %reduce-scatter.2.cloned.1.call-done = bf16[2,512,2048]{2,1,0:T(8,128)(2,1)} async-done(((bf16[2,1024,2048]{2,1,0:T(8,128)(2,1)}), bf16[2,512,2048]{2,1,0:T(8,128)(2,1)}) %reduce-scatter.2.cloned.1.call-update) | async-done | bytes 4194320 | tf_op jit(solution)/shard_map/reduce_scatter | solution.py:23
  229.4 6.7 %convert_element_type.4 = f32[2,512,2048]{2,1,0:T(8,128)} convert(bf16[2,512,2048]{2,1,0:T(8,128)(2,1)} %reduce-scatter.2.cloned.1.call-done) | non-fusion elementwise | flops 2097152 | bytes 12582912 | tf_op jit(solution)/shard_map/convert_element_type | solution.py:25
Async XLA Ops:
  6.5 52.9 %all-gather.3.cloned.1.call-start = ((), (), s32[]{:S(2)}) async-start(), calls=%async_computation.2 | async-start | bytes 2359296 | tf_op jit(solution)/shard_map/all_gather | solution.py:18
  19.9 83.8 %all-gather.5.cloned.1.call-start = ((), (), s32[]{:S(2)}) async-start(), calls=%async_computation.3 | async-start | bytes 4456448 | tf_op jit(solution)/shard_map/all_gather | solution.py:21
  20.7 208.7 %reduce-scatter.2.cloned.1.call-start = ((), (), s32[]{:S(2)}) async-start(), calls=%async_computation.4 | async-start | bytes 12582912 | tf_op jit(solution)/shard_map/reduce_scatter | solution.py:23
  103.8 2.6 %copy-start = (bf16[1024,512]{1,0:T(8,128)(2,1)S(1)}, bf16[1024,512]{1,0:T(8,128)(2,1)}, u32[]{:S(2)}) copy-start(bf16[1024,512]{1,0:T(8,128)(2,1)} %get-tuple-element.7) | copy-start | bytes 3145732
Sparse Core Ops, SparseCore 0:
  20.1 39.2 all-gather.2
  61.2 42.4 all-gather.4
  123.8 105.5 reduce-scatter.1
where the time goes:
time: 243 us
  waiting for transfers between devices  186 us (77%)
  other arithmetic  14.3 us (6%)
  between operations  13.2 us (5%)
  matrix products  10.9 us (4%)
  blocking collectives  10.3 us (4%)
  local copies, waits for them, and re-layouts  8.25 us (3%)
    reduce_scatter x1, waiting for transfers between devices, body(): lax.psum_scatter(terms.astype(jnp.bfloat16), 'slab', scatter_dimension=1,...  106 us
    all_gather x1, waiting for transfers between devices, body(): column_set = lax.all_gather(local, 'row', axis=1, tiled=True)  40.4 us
    all_gather x1, waiting for transfers between devices, body(): row_block = lax.all_gather(local, 'col', axis=1, tiled=True)  38.7 us
    all_to_all x1, blocking collectives, body(): lax.all_to_all(fields, 'slab', split_axis=2, concat_axis=1, tiled=True)  10.3 us
    convert_element_type x1, other arithmetic, body(): gram = lax.psum_scatter(terms.astype(jnp.bfloat16), 'slab', scatter_dimen...  6.65 us
    another operation x1, other arithmetic, pair_terms(): return jnp.stack([real, imag])  6.35 us
    dot_general x1, matrix products, pair_terms(): lax.dot_general(left_imag, right_imag, dims, preferred_element_type=jnp.f...  6.13 us
  transfers between devices with their start and end apart: 3, of which 3 were waited for; matrix products, arithmetic and copies ran while one was open for 2% of the time, Pallas kernels for 0%

commit v1 on v0

--- a/solution.py
+++ b/solution.py
@@ -2,6 +2,22 @@
 import jax.numpy as jnp
 from jax import lax
 from jax.sharding import PartitionSpec as P
+
+
+def gather_around(x, axis, dim):
+    ways, here, hop = (lax.axis_size(axis), lax.axis_index(axis), x.shape[dim])
+    dims = [n * ways if d == dim else n for d, n in enumerate(x.shape)]
+    full = lax.dynamic_update_slice_in_dim(jnp.zeros(dims, x.dtype), x, here * hop, axis=dim)
+    going_up = going_down = x
+    for far in range(1, ways // 2 + 1):
+        going_up = lax.ppermute(going_up, axis, [(d, (d + 1) % ways) for d in range(ways)])
+        full = lax.dynamic_update_slice_in_dim(full, going_up, (here - far) % ways * hop, axis=dim)
+        if 2 * far < ways:
+            going_down = lax.ppermute(going_down, axis, [(d, (d - 1) % ways) for d in range(ways)])
+            full = lax.dynamic_update_slice_in_dim(
+                full, going_down, (here + far) % ways * hop, axis=dim
+            )
+    return full
 
 
 def pair_terms(left_real, left_imag, piece):
@@ -15,7 +31,7 @@
 
 def body(fields):
     local = lax.all_to_all(fields, "slab", split_axis=2, concat_axis=1, tiled=True)
-    row_block = lax.all_gather(local, "col", axis=1, tiled=True)
+    row_block = gather_around(local, "col", 1)
     left_real = jnp.concatenate([row_block[0], row_block[1]], axis=1)
     left_imag = jnp.concatenate([row_block[0], -row_block[1]], axis=1)
     column_set = lax.all_gather(local, "row", axis=1, tiled=True)

time: 243 us -> 202 us (0.83)
  waiting for transfers between devices: 186 us -> 135 us
  starting transfers between devices: 0.08 us -> 11.2 us
    all_gather x1 -> x0, waiting for transfers between devices: 38.7 us -> none  [body(): row_block = lax.all_gather(local, 'col', axis=1, tiled=True)]
    all_gather x1, waiting for transfers between devices: 40.4 us -> 10.6 us  [body(): column_set = lax.all_gather(local, 'row', axis=1, tiled=True)]
    ppermute x0 -> x7, waiting for transfers between devices: none -> 18.9 us  [the longest x4 18.8 us: gather_around(): lax.ppermute(going_up, axis, [(d, (d + 1) % ways) for d in range(ways)])]
    ppermute x0 -> x7, starting transfers between devices: none -> 11.2 us  [the longest x3 9.45 us: gather_around(): lax.ppermute(going_down, axis, [(d, (d - 1) % ways) for d in range(ways)])]
  transfers between devices with their start and end apart: 3 -> 9, of which waited for: 3 -> 6; matrix products, arithmetic and copies ran while one was open for 2% -> 1% of each run, Pallas kernels for 0% -> 0%
where the time goes in v1:
time: 202 us; the launch traced here: 201 us
  waiting for transfers between devices  135 us (67%)
  between operations  13.5 us (7%)
  other arithmetic  13.1 us (6%)
  starting transfers between devices  11.2 us (6%)
  matrix products  10.9 us (5%)
  blocking collectives  10.3 us (5%)
  local copies, waits for them, and re-layouts  7.07 us (4%)
    reduce_scatter x1, waiting for transfers between devices, body(): lax.psum_scatter(terms.astype(jnp.bfloat16), 'slab', scatter_dimension=1,...  106 us
    ppermute x4, waiting for transfers between devices, gather_around(): lax.ppermute(going_up, axis, [(d, (d + 1) % ways) for d in range(ways)])  18.8 us
    all_gather x1, waiting for transfers between devices, body(): column_set = lax.all_gather(local, 'row', axis=1, tiled=True)  10.6 us
    all_to_all x1, blocking collectives, body(): lax.all_to_all(fields, 'slab', split_axis=2, concat_axis=1, tiled=True)  10.3 us
    ppermute x3, starting transfers between devices, gather_around(): lax.ppermute(going_down, axis, [(d, (d - 1) % ways) for d in range(ways)])  9.45 us
    convert_element_type x1, other arithmetic, body(): gram = lax.psum_scatter(terms.astype(jnp.bfloat16), 'slab', scatter_dimen...  6.65 us
    another operation x1, other arithmetic, pair_terms(): return jnp.stack([real, imag])  6.35 us
    dot_general x1, matrix products, pair_terms(): lax.dot_general(left_imag, right_imag, dims, preferred_element_type=jnp.f...  6.12 us
  transfers between devices with their start and end apart: 9, of which 6 were waited for; matrix products, arithmetic and copies ran while one was open for 1% of the time, Pallas kernels for 0%

profile of v1, /device:TPU:1, one launch (start us, length us, event | category | flops | bytes accessed | tf_op | source)
XLA Modules:
  0.0 201.4 jit_solution(10168267526684357244)
XLA Ops:
  6.5 1.3 copy.3
  7.8 0.4 reshape
  8.2 10.3 %all_to_all.18 = bf16[2,2,32768]{2,1,0:T(2,128)(2,1)S(1)} all-to-all(bf16[2,2,32768]{2,1,0:T(2,128)(2,1)S(1)} %reshape), channel_id=1, replica_groups=mesh['row'=16,'col'=8,'slab'=2] {'slab'}, dimensions={0} | all-to-all | bytes 524288 | tf_op jit(solution)/shard_map/all_to_all | solution.py:33
  18.6 0.3 reshape.1
  18.9 1.0 copy.5
  20.0 0.0 all-gather.2.cloned.1.call-update
  20.0 0.0 reduce-scatter.2.cloned.1.call-start
  20.0 1.7 collective-permute-start
  21.7 4.0 %collective-permute-start.1 = (bf16[2,128,512]{2,1,0:T(8,128)(2,1)}, bf16[2,128,512]{2,1,0:T(8,128)(2,1)S(1)}, u32[]{:S(2)}, u32[]{:S(2)}) collective-permute-start(bf16[2,128,512]{2,1,0:T(8,128)(2,1)} %bitcast.23), channel_id=1, source_target_pairs={{0,14},{2,0},{4,2},{6,4},{8,6},{10,8},{12,10},{14,12},{1,15},{3,1}... | collective-permute-start | bytes 786440 | tf_op jit(solution)/shard_map/ppermute | solution.py:16
  25.8 4.6 %collective-permute-done = bf16[2,128,512]{2,1,0:T(8,128)(2,1)S(1)} collective-permute-done((bf16[2,128,512]{2,1,0:T(8,128)(2,1)}, bf16[2,128,512]{2,1,0:T(8,128)(2,1)S(1)}, u32[]{:S(2)}, u32[]{:S(2)}) %collective-permute-start) | collective-permute-done | bytes 262176 | tf_op jit(solution)/shard_map/ppermute | solution.py:13
  30.4 0.0 collective-permute-start.2
  30.4 0.0 collective-permute-done.1
  30.4 2.7 %collective-permute-start.3 = (bf16[2,128,512]{2,1,0:T(8,128)(2,1)S(1)}, bf16[2,128,512]{2,1,0:T(8,128)(2,1)S(1)}, u32[]{:S(2)}, u32[]{:S(2)}) collective-permute-start(bf16[2,128,512]{2,1,0:T(8,128)(2,1)S(1)} %collective-permute-done.1), channel_id=1, source_target_pairs={{0,14},{2,0},{4,2},{6,4},{8,6},{10,8},{12,10},{14,12},{1,15},{3,1}... | collective-permute-start | bytes 786440 | tf_op jit(solution)/shard_map/ppermute | solution.py:16
  33.1 0.1 broadcast_in_dim.3
  33.3 3.6 %collective-permute-done.2 = bf16[2,128,512]{2,1,0:T(8,128)(2,1)S(1)} collective-permute-done((bf16[2,128,512]{2,1,0:T(8,128)(2,1)S(1)}, bf16[2,128,512]{2,1,0:T(8,128)(2,1)S(1)}, u32[]{:S(2)}, u32[]{:S(2)}) %collective-permute-start.2) | collective-permute-done | bytes 262176 | tf_op jit(solution)/shard_map/ppermute | solution.py:13
  36.8 0.0 collective-permute-start.4
  36.9 0.0 collective-permute-done.3
  36.9 2.7 %collective-permute-start.5 = (bf16[2,128,512]{2,1,0:T(8,128)(2,1)S(1)}, bf16[2,128,512]{2,1,0:T(8,128)(2,1)S(1)}, u32[]{:S(2)}, u32[]{:S(2)}) collective-permute-start(bf16[2,128,512]{2,1,0:T(8,128)(2,1)S(1)} %collective-permute-done.3), channel_id=1, source_target_pairs={{0,14},{2,0},{4,2},{6,4},{8,6},{10,8},{12,10},{14,12},{1,15},{3,1}... | collective-permute-start | bytes 786440 | tf_op jit(solution)/shard_map/ppermute | solution.py:16
  39.7 3.6 %collective-permute-done.4 = bf16[2,128,512]{2,1,0:T(8,128)(2,1)S(1)} collective-permute-done((bf16[2,128,512]{2,1,0:T(8,128)(2,1)S(1)}, bf16[2,128,512]{2,1,0:T(8,128)(2,1)S(1)}, u32[]{:S(2)}, u32[]{:S(2)}) %collective-permute-start.4) | collective-permute-done | bytes 262176 | tf_op jit(solution)/shard_map/ppermute | solution.py:13
  43.3 0.0 collective-permute-start.6
  43.3 0.0 collective-permute-done.5
  43.4 7.1 %collective-permute-done.6 = bf16[2,128,512]{2,1,0:T(8,128)(2,1)S(1)} collective-permute-done((bf16[2,128,512]{2,1,0:T(8,128)(2,1)S(1)}, bf16[2,128,512]{2,1,0:T(8,128)(2,1)S(1)}, u32[]{:S(2)}, u32[]{:S(2)}) %collective-permute-start.6) | collective-permute-done | bytes 262176 | tf_op jit(solution)/shard_map/ppermute | solution.py:13
  50.5 0.1 fusion.16
  50.5 1.1 slice_bitcast_fusion.2
  51.6 10.6 %all-gather.2.cloned.1.call-done = bf16[2,2048,512]{2,1,0:T(8,128)(2,1)} async-done(((bf16[2,128,512]{2,1,0:T(8,128)(2,1)}), bf16[2,2048,512]{2,1,0:T(8,128)(2,1)}) %all-gather.2.cloned.1.call-update) | async-done | bytes 4194320 | tf_op jit(solution)/shard_map/all_gather | solution.py:37
  62.3 2.6 %slice_bitcast_fusion = (bf16[2048,512]{1,0:T(8,128)(2,1)S(1)}, bf16[2048,512]{1,0:T(8,128)(2,1)S(1)}) fusion(bf16[2,2048,512]{2,1,0:T(8,128)(2,1)} %all-gather.2.cloned.1.call-done), kind=kLoop, calls=%fused_computation.13 | loop fusion | bytes 8388608 | tf_op jit(solution)/shard_map/squeeze | solution.py:24
  64.9 4.8 %convert_bitcast_fusion.1 = bf16[1,1024,2048]{2,1,0:T(8,128)(2,1)S(1)} fusion(bf16[2048,512]{1,0:T(8,128)(2,1)S(1)} %get-tuple-element.5, bf16[2048,512]{1,0:T(8,128)(2,1)S(1)} %get-tuple-element.6, bf16[1024,512]{1,0:T(8,128)(2,1)S(1)} %get-tuple-element.8, bf16[1024,512]{1,0:T(8,128)(2,1)S(1)} %copy-done.1), kind=kOutput, calls=%fused_computation.10 | convolution fusion | flops 4309647360 | bytes 10485760 | tf_op jit(solution)/shard_map/dot_general | solution.py:27
  69.7 6.1 %convert_bitcast_fusion = bf16[1,1024,2048]{2,1,0:T(8,128)(2,1)} fusion(bf16[2048,512]{1,0:T(8,128)(2,1)S(1)} %get-tuple-element.6, bf16[2048,512]{1,0:T(8,128)(2,1)S(1)} %get-tuple-element.5, bf16[1024,512]{1,0:T(8,128)(2,1)S(1)} %get-tuple-element.8, bf16[1024,512]{1,0:T(8,128)(2,1)S(1)} %fusion.16), kind=kOutput, calls=%fused_computation.9 | convolution fusion | flops 4309647360 | bytes 10485760 | tf_op jit(solution)/shard_map/dot_general | solution.py:28
  75.8 6.3 %pad_maximum_fusion = bf16[2,1024,2048]{2,1,0:T(8,128)(2,1)} fusion(bf16[1,1024,2048]{2,1,0:T(8,128)(2,1)} %convert_bitcast_fusion, bf16[1,1024,2048]{2,1,0:T(8,128)(2,1)S(1)} %convert_bitcast_fusion.1), kind=kLoop, calls=%fused_computation | loop fusion | flops 4194304 | bytes 16777216 | tf_op jit(solution)/shard_map/stack | solution.py:29
  82.1 0.0 reduce-scatter.2.cloned.1.call-update
  82.1 105.8 %reduce-scatter.2.cloned.1.call-done = bf16[2,512,2048]{2,1,0:T(8,128)(2,1)} async-done(((bf16[2,1024,2048]{2,1,0:T(8,128)(2,1)}), bf16[2,512,2048]{2,1,0:T(8,128)(2,1)}) %reduce-scatter.2.cloned.1.call-update) | async-done | bytes 4194320 | tf_op jit(solution)/shard_map/reduce_scatter | solution.py:39
  187.9 6.7 %convert_element_type.4 = f32[2,512,2048]{2,1,0:T(8,128)} convert(bf16[2,512,2048]{2,1,0:T(8,128)(2,1)} %reduce-scatter.2.cloned.1.call-done) | non-fusion elementwise | flops 2097152 | bytes 12582912 | tf_op jit(solution)/shard_map/convert_element_type | solution.py:41
  (13 shorter events, 0.2 us)
Async XLA Ops:
  6.5 55.7 %all-gather.2.cloned.1.call-start = ((), (), s32[]{:S(2)}) async-start(), calls=%async_computation.2 | async-start | bytes 4456448 | tf_op jit(solution)/shard_map/all_gather | solution.py:37
  20.0 13.3 %copy-start = (bf16[2,2,64,512]{3,2,1,0:T(8,128)(2,1)S(1)}, bf16[2,2,64,512]{3,2,1,0:T(8,128)(2,1)}, u32[]{:S(2)}) copy-start(bf16[2,2,64,512]{3,2,1,0:T(8,128)(2,1)} %copy.5) | copy-start | bytes 786436
  20.0 167.9 %reduce-scatter.2.cloned.1.call-start = ((), (), s32[]{:S(2)}) async-start(), calls=%async_computation.3 | async-start | bytes 12582912 | tf_op jit(solution)/shard_map/reduce_scatter | solution.py:39
  20.0 10.4 %collective-permute-start = (bf16[2,128,512]{2,1,0:T(8,128)(2,1)}, bf16[2,128,512]{2,1,0:T(8,128)(2,1)S(1)}, u32[]{:S(2)}, u32[]{:S(2)}) collective-permute-start(bf16[2,128,512]{2,1,0:T(8,128)(2,1)} %bitcast.22), channel_id=1, source_target_pairs={{0,2},{2,4},{4,6},{6,8},{8,10},{10,12},{12,14},{14,0},{1,3},{3,5},... | collective-permute-start | bytes 786440 | tf_op jit(solution)/shard_map/ppermute | solution.py:13
  21.7 8.7 %collective-permute-start.1 = (bf16[2,128,512]{2,1,0:T(8,128)(2,1)}, bf16[2,128,512]{2,1,0:T(8,128)(2,1)S(1)}, u32[]{:S(2)}, u32[]{:S(2)}) collective-permute-start(bf16[2,128,512]{2,1,0:T(8,128)(2,1)} %bitcast.23), channel_id=1, source_target_pairs={{0,14},{2,0},{4,2},{6,4},{8,6},{10,8},{12,10},{14,12},{1,15},{3,1}... | collective-permute-start | bytes 786440 | tf_op jit(solution)/shard_map/ppermute | solution.py:16
  30.4 6.4 %collective-permute-start.2 = (bf16[2,128,512]{2,1,0:T(8,128)(2,1)S(1)}, bf16[2,128,512]{2,1,0:T(8,128)(2,1)S(1)}, u32[]{:S(2)}, u32[]{:S(2)}) collective-permute-start(bf16[2,128,512]{2,1,0:T(8,128)(2,1)S(1)} %collective-permute-done), channel_id=1, source_target_pairs={{0,2},{2,4},{4,6},{6,8},{8,10},{10,12},{12,14},{14,0},{1,3},{3,5},... | collective-permute-start | bytes 786440 | tf_op jit(solution)/shard_map/ppermute | solution.py:13
  30.4 6.5 %collective-permute-start.3 = (bf16[2,128,512]{2,1,0:T(8,128)(2,1)S(1)}, bf16[2,128,512]{2,1,0:T(8,128)(2,1)S(1)}, u32[]{:S(2)}, u32[]{:S(2)}) collective-permute-start(bf16[2,128,512]{2,1,0:T(8,128)(2,1)S(1)} %collective-permute-done.1), channel_id=1, source_target_pairs={{0,14},{2,0},{4,2},{6,4},{8,6},{10,8},{12,10},{14,12},{1,15},{3,1}... | collective-permute-start | bytes 786440 | tf_op jit(solution)/shard_map/ppermute | solution.py:16
  36.8 6.4 %collective-permute-start.4 = (bf16[2,128,512]{2,1,0:T(8,128)(2,1)S(1)}, bf16[2,128,512]{2,1,0:T(8,128)(2,1)S(1)}, u32[]{:S(2)}, u32[]{:S(2)}) collective-permute-start(bf16[2,128,512]{2,1,0:T(8,128)(2,1)S(1)} %collective-permute-done.2), channel_id=1, source_target_pairs={{0,2},{2,4},{4,6},{6,8},{8,10},{10,12},{12,14},{14,0},{1,3},{3,5},... | collective-permute-start | bytes 786440 | tf_op jit(solution)/shard_map/ppermute | solution.py:13
  36.9 6.4 %collective-permute-start.5 = (bf16[2,128,512]{2,1,0:T(8,128)(2,1)S(1)}, bf16[2,128,512]{2,1,0:T(8,128)(2,1)S(1)}, u32[]{:S(2)}, u32[]{:S(2)}) collective-permute-start(bf16[2,128,512]{2,1,0:T(8,128)(2,1)S(1)} %collective-permute-done.3), channel_id=1, source_target_pairs={{0,14},{2,0},{4,2},{6,4},{8,6},{10,8},{12,10},{14,12},{1,15},{3,1}... | collective-permute-start | bytes 786440 | tf_op jit(solution)/shard_map/ppermute | solution.py:16
  43.3 7.2 %collective-permute-start.6 = (bf16[2,128,512]{2,1,0:T(8,128)(2,1)S(1)}, bf16[2,128,512]{2,1,0:T(8,128)(2,1)S(1)}, u32[]{:S(2)}, u32[]{:S(2)}) collective-permute-start(bf16[2,128,512]{2,1,0:T(8,128)(2,1)S(1)} %collective-permute-done.4), channel_id=1, source_target_pairs={{0,2},{2,4},{4,6},{6,8},{8,10},{10,12},{12,14},{14,0},{1,3},{3,5},... | collective-permute-start | bytes 786440 | tf_op jit(solution)/shard_map/ppermute | solution.py:13
  62.3 2.6 %copy-start.1 = (bf16[1024,512]{1,0:T(8,128)(2,1)S(1)}, bf16[1024,512]{1,0:T(8,128)(2,1)}, u32[]{:S(2)}) copy-start(bf16[1024,512]{1,0:T(8,128)(2,1)} %get-tuple-element.7) | copy-start | bytes 3145732
Sparse Core Ops, SparseCore 0:
  20.1 42.1 all-gather.1
  82.3 105.5 reduce-scatter.1
